TPU v7x, 32 devices: a whole 2x2x4 slice. The times are simulated.
32 devices in a mesh: groups: 2 (over y), row: 8 (over z, x), col: 2 (over core).
Axes of the slice: x: 2, y: 2, z: 4, core: 2. Of those that a mesh axis runs over, the one named last changes fastest.
Arguments:
- embeddings: bfloat16 [128, 16, 1280], P(('groups', 'row'), 'col'), parts along dimension 0, may hold values from -6 to 52
- pos_embed: bfloat16 [256, 1280], replicated, may hold values from -3 to 3
- ln_gain: float32 [1280], replicated, may hold values from 0.6 to 9
- ln_bias: float32 [1280], replicated, may hold values from -1.5 to 1.5
- w_qkv: bfloat16 [1280, 1920], P(('row', 'col')), may hold values from -0.25155765 to 0.25155765
- b_qkv: float32 [1920], replicated, may hold values from -1.5 to 1.5
- w_out: bfloat16 [1280, 640], P(('row', 'col')), may hold values from -0.25 to 0.25
- b_out: float32 [1280], replicated, may hold values from -1.5 to 1.5
- valid: int32 [16, 2, 256], P(('groups', 'row'), 'col'), parts along dimension 0, may hold values from 0 to 196
Outputs:
- merged: bfloat16 [128, 16, 1280], P(('groups', 'row'), 'col'), parts along dimension 0
There are 2 independent parts, one for each index of `groups`. A program takes and returns all parts, laid end to end along the dimension named above; an argument that names none is the same for every part. Nothing has to cross between parts.
All inputs are finite; a program needn't handle non-finite values.
Results may differ from a plain program's by a relative error of at most 0.0098.
Values may be sent and summed in bfloat16 or wider, within the bound.
A program may use at most 64 MiB of HBM per device.

v0:
```python
import jax
import jax.numpy as jnp
from jax import lax
from jax.sharding import PartitionSpec as P

HEADS = 8
EPSILON = 1e-06
SPREAD = 4.0
FLOOR = 0.25


def shifted(value, axis, steps):
    count = lax.axis_size(axis)
    initial, last = (max(0, -steps), min(count, count - steps))
    return lax.ppermute(value, axis, [(source, source + steps) for source in range(initial, last)])


def extended(block, sides, width):
    for axis, dim in sides:
        count = lax.axis_size(axis)
        forward = [(i, i + 1) for i in range(count - 1)]
        backward = [(target, source) for source, target in forward]
        low = lax.ppermute(
            lax.slice_in_dim(block, block.shape[dim] - width, None, axis=dim), axis, forward
        )
        high = lax.ppermute(lax.slice_in_dim(block, 0, width, axis=dim), axis, backward)
        block = jnp.concatenate([low, block, high], axis=dim)
    return block


def layer_norm(inputs, ln_gain, ln_bias):
    centred = inputs - jnp.mean(inputs, axis=-1, keepdims=True)
    variance = jnp.mean(centred * centred, axis=-1, keepdims=True)
    return centred * lax.rsqrt(variance + EPSILON) * ln_gain + ln_bias


def gauss_table(win):
    offsets = jnp.arange(win, dtype=jnp.float32) - (win - 1) / 2.0
    squared = offsets[:, None] * offsets[:, None] + offsets[None, :] * offsets[None, :]
    return jnp.exp(-squared / (2.0 * SPREAD * SPREAD))


def attend(projected):
    rows_count = projected.shape[0]
    width = projected.shape[1] // 3
    head_size = width // HEADS
    queries = projected[:, :width].reshape(rows_count, HEADS, head_size)
    keys = projected[:, width : 2 * width].reshape(rows_count, HEADS, head_size)
    values = projected[:, 2 * width :].reshape(rows_count, HEADS, head_size)
    scores = jnp.einsum(
        "qhd,khd->hqk", queries, keys, preferred_element_type=jnp.float32
    ) * head_size ** (-0.5)
    highest = jnp.max(scores, axis=-1, keepdims=True)
    expon = jnp.exp(scores - highest)
    probs = (expon / jnp.sum(expon, axis=-1, keepdims=True)).astype(jnp.bfloat16)
    mixed = jnp.einsum("hqk,khd->qhd", probs, values, preferred_element_type=jnp.float32)
    return mixed.astype(jnp.bfloat16).reshape(rows_count, width)


def fold_rows(numerator, denominator, rim):
    from_next = (
        shifted(numerator[:rim].astype(jnp.bfloat16), "row", -1).astype(jnp.float32),
        shifted(denominator[:rim].astype(jnp.bfloat16), "row", -1).astype(jnp.float32),
    )
    from_prev = (
        shifted(numerator[-rim:].astype(jnp.bfloat16), "row", 1).astype(jnp.float32),
        shifted(denominator[-rim:].astype(jnp.bfloat16), "row", 1).astype(jnp.float32),
    )
    middle_num = numerator[rim:-rim]
    middle_den = denominator[rim:-rim]
    middle_num = middle_num.at[:rim].add(from_prev[0]).at[-rim:].add(from_next[0])
    middle_den = middle_den.at[:rim].add(from_prev[1]).at[-rim:].add(from_next[1])
    return (middle_num, middle_den)


def fold_cols(numerator, denominator, rim):
    from_next = (
        shifted(numerator[:, :rim].astype(jnp.bfloat16), "col", -1).astype(jnp.float32),
        shifted(denominator[:, :rim].astype(jnp.bfloat16), "col", -1).astype(jnp.float32),
    )
    from_prev = (
        shifted(numerator[:, -rim:].astype(jnp.bfloat16), "col", 1).astype(jnp.float32),
        shifted(denominator[:, -rim:].astype(jnp.bfloat16), "col", 1).astype(jnp.float32),
    )
    middle_num = numerator[:, rim:-rim] + jnp.concatenate([from_prev[0], from_next[0]], axis=1)
    middle_den = denominator[:, rim:-rim] + jnp.concatenate([from_prev[1], from_next[1]], axis=1)
    return (middle_num, middle_den)


def body(embeddings, pos_embed, ln_gain, ln_bias, w_qkv, b_qkv, w_out, b_out, valid):
    tile = embeddings.shape[1]
    tile_rows = embeddings.shape[0] // tile
    rim = tile // 2
    win = tile + 2 * rim
    rows_count = win * win
    width_model = embeddings.shape[2]
    window = extended(embeddings, (("row", 0), ("col", 1)), rim)
    stacked = jnp.stack([window], axis=0)
    inputs = stacked.reshape(tile_rows, rows_count, width_model).astype(
        jnp.float32
    ) + pos_embed.astype(jnp.float32)
    inputs = inputs.reshape(tile_rows * rows_count, width_model)
    normed = layer_norm(inputs, ln_gain, ln_bias).astype(jnp.bfloat16)
    projected = jnp.dot(
        normed,
        lax.all_gather(w_qkv, ("row", "col"), axis=0, tiled=True),
        preferred_element_type=jnp.float32,
    )
    projected = (
        (projected + b_qkv).astype(jnp.bfloat16).reshape(tile_rows, rows_count, w_qkv.shape[1])
    )
    attended = jax.vmap(attend)(projected).reshape(tile_rows * rows_count, -1)
    projected_out = lax.dot_general(
        attended,
        lax.all_gather(w_out, ("row", "col"), axis=0, tiled=True),
        (((1,), (1,)), ((), ())),
        preferred_element_type=jnp.float32,
    )
    hidden = inputs + projected_out + b_out
    gauss = gauss_table(win).reshape(1, rows_count)
    weight = gauss * valid.reshape(tile_rows, rows_count).astype(jnp.float32) / 196.0
    contrib = (weight.reshape(tile_rows * rows_count, 1) * hidden).reshape(
        tile_rows, win, win, width_model
    )
    weight_grid = weight.reshape(tile_rows, win, win)
    numerator = jnp.zeros((tile_rows * tile + 2 * rim, win, width_model), jnp.float32)
    denominator = jnp.zeros((tile_rows * tile + 2 * rim, win), jnp.float32)
    numerator = numerator.at[0:win].add(contrib[0])
    denominator = denominator.at[0:win].add(weight_grid[0])
    numerator, denominator = fold_rows(numerator, denominator, rim)
    numerator, denominator = fold_cols(numerator, denominator, rim)
    return (numerator / jnp.maximum(denominator, FLOOR)[:, :, None]).astype(jnp.bfloat16)


def solution(mesh):
    placed = (
        P(("groups", "row"), "col", None),
        P(),
        P(),
        P(),
        P(("row", "col"), None),
        P(),
        P(("row", "col"), None),
        P(),
        P(("groups", "row"), "col", None),
    )
    return jax.shard_map(
        body,
        mesh=mesh,
        in_specs=placed,
        out_specs=P(("groups", "row"), "col", None),
        check_vma=False,
    )
```

profile of v0, /device:TPU:0, one launch (start us, length us, event | category | flops | bytes accessed | tf_op | source)
XLA Modules:
  0.0 136.9 jit_solution(5850899575125565786)
XLA Ops:
  6.5 0.0 all-gather.3.cloned.1.call-start
  6.5 0.7 all-gather.3.cloned.1.call-update
  7.3 0.0 all-gather.5.cloned.1.call-start
  7.3 0.9 fusion.25
  8.2 4.9 %collective-permute-start = (bf16[4,8,1280]{2,1,0:T(8,128)(2,1)S(1)}, bf16[4,8,1280]{2,1,0:T(8,128)(2,1)S(1)}, u32[]{:S(2)}, u32[]{:S(2)}) collective-permute-start(bf16[4,8,1280]{2,1,0:T(8,128)(2,1)S(1)} %get-tuple-element.105), channel_id=1, source_target_pairs={{0,2},{2,4},{4,6},{6,8},{8,10},{10,12},{12,14},{1,3},{3,5},{5,7},{... | collective-permute-start | bytes 245768 | tf_op jit(solution)/shard_map/ppermute | solution.py:23
  13.1 1.3 collective-permute-start.1
  14.4 0.7 convert_reduce_fusion
  15.1 0.1 convert_element_type.105
  15.2 0.1 fusion.20
  15.3 4.5 %collective-permute-start.8 = (bf16[4,16]{1,0:T(4,128)(2,1)S(1)}, bf16[4,16]{1,0:T(4,128)(2,1)S(1)}, u32[]{:S(2)}, u32[]{:S(2)}) collective-permute-start(bf16[4,16]{1,0:T(4,128)(2,1)S(1)} %get-tuple-element.107), channel_id=1, source_target_pairs={{0,2},{2,4},{4,6},{6,8},{8,10},{10,12},{12,14},{1,3},{3,5},{5,7},{... | collective-permute-start | bytes 392 | tf_op jit(solution)/shard_map/ppermute | solution.py:15
  19.9 1.3 collective-permute-start.9
  21.2 0.0 all-gather.5.cloned.1.call-update
  21.2 0.1 multiply_exponential_fusion
  21.3 0.7 convert_element_type.90
  22.0 0.1 exp.26
  22.0 0.0 collective-permute-done.8
  22.1 0.0 copy-start
  22.1 0.0 collective-permute-done
  22.1 1.0 constant_dynamic-update-slice_fusion.1
  23.1 0.0 collective-permute-done.1
  23.1 0.1 fusion.24
  23.2 1.3 collective-permute-start.2
  24.6 1.3 collective-permute-start.3
  25.9 0.1 collective-permute-done.9
  25.9 0.0 collective-permute-done.2
  25.9 1.9 %collective-permute-done.3 = bf16[16,4,1280]{2,1,0:T(4,128)(2,1)S(1)} collective-permute-done((bf16[16,4,1280]{2,1,0:T(4,128)(2,1)S(1)}, bf16[16,4,1280]{2,1,0:T(4,128)(2,1)S(1)}, u32[]{:S(2)}, u32[]{:S(2)}) %collective-permute-start.3) | collective-permute-done | bytes 163872 | tf_op jit(solution)/shard_map/ppermute | solution.py:26
  27.8 0.3 pad_maximum_fusion
  28.2 0.0 copy-done
  28.2 0.0 copy-start.2
  28.2 0.0 copy-start.3
  28.2 0.0 copy-start.4
  28.2 0.3 fusion.6
  28.5 0.4 multiply_reduce_fusion.1
  28.9 37.5 %all-gather.3.cloned.1.call-done = bf16[1280,1920]{1,0:T(8,128)(2,1)} async-done(((bf16[80,1920]{1,0:T(8,128)(2,1)}), bf16[1280,1920]{1,0:T(8,128)(2,1)}) %all-gather.3.cloned.1.call-update) | async-done | bytes 4915216 | tf_op jit(solution)/shard_map/all_gather | solution.py:106
  66.4 0.0 copy-done.2
  66.4 0.0 copy-done.3
  66.4 0.0 copy-done.4
  66.4 4.1 %fusion.4 = bf16[1,256,1920]{2,1,0:T(8,128)(2,1)S(1)} fusion(bf16[1280,1920]{1,0:T(8,128)(2,1)} %all-gather.3.cloned.1.call-done, f32[1920]{0:T(1024)S(1)} %copy-done.2, bf16[256,1280]{1,0:T(8,128)(2,1)S(1)} %copy-done, bf16[256,1280]{1,0:T(8,128)(2,1)S(1)} %bitcast.37, f32[1280]{0:T(1024)S(1)} %copy-done.3, f32[1280]{0:T(1024)S(1)} %copy-done.4, ...), kind=kOutput, calls=%fused_computation.6 | convolution fusion | flops 1261895680 | bytes 7228928 | tf_op jit(solution)/shard_map/dot_general | solution.py:104
  70.5 0.1 fusion.21
  70.6 0.2 copy.15
  70.8 0.2 copy.16
  71.0 0.2 copy.14
  71.2 2.2 %fusion.27 = (f32[8,256]{1,0:T(8,128)S(1)}, f32[8,256,256]{1,2,0:T(8,128)}) fusion(bf16[256,8,80]{0,2,1:T(8,128)(2,1)S(1)} %bitcast.42, bf16[256,8,80]{0,2,1:T(8,128)(2,1)S(1)} %bitcast.43), kind=kOutput, calls=%fused_computation.55 | convolution fusion | flops 85459200 | bytes 2760704 | tf_op jit(solution)/shard_map/vmap()/sub | solution.py:54
  73.3 2.0 %convolution_convert_fusion = bf16[8,80,256]{2,1,0:T(8,128)(2,1)S(1)} fusion(bf16[256,8,80]{0,2,1:T(8,128)(2,1)S(1)} %bitcast.44, f32[8,256,256]{1,2,0:T(8,128)} %get-tuple-element.111, f32[8,256]{1,0:T(8,128)S(1)} %get-tuple-element.110), kind=kOutput, calls=%fused_computation.14 | convolution fusion | flops 85098496 | bytes 2760704 | tf_op jit(solution)/shard_map/vmap(hqk,khd->qhd)/dot_general | solution.py:56
  75.3 31.7 %all-gather.5.cloned.1.call-done = bf16[1280,640]{1,0:T(8,128)(2,1)} async-done(((bf16[80,640]{1,0:T(8,128)(2,1)}), bf16[1280,640]{1,0:T(8,128)(2,1)}) %all-gather.5.cloned.1.call-update) | async-done | bytes 1638416 | tf_op jit(solution)/shard_map/all_gather | solution.py:115
  107.0 0.0 copy-done.1
  107.0 2.3 %fusion.28 = (bf16[256,1280]{1,0:T(8,128)(2,1)S(1)}, f32[256,1280]{1,0:T(8,128)S(1)}) fusion(f32[1280]{0:T(1024)S(1)} %copy-done.1, bf16[256,640]{0,1:T(8,128)(2,1)S(1)} %bitcast.41, bf16[1280,640]{1,0:T(8,128)(2,1)} %all-gather.5.cloned.1.call-done, bf16[256,1280]{1,0:T(8,128)(2,1)S(1)} %copy-done, bf16[256,1280]{1,0:T(8,128)(2,1)S(1)} %bitcast.38, ...), kind=kOutput, calls=%fused_computation.56 | convolution fusion | flops 421724160 | bytes 5249024 | tf_op jit(solution)/shard_map/dot_general | solution.py:113
  109.3 2.4 %collective-permute-start.4 = (bf16[4,16,1280]{2,1,0:T(8,128)(2,1)S(1)}, bf16[4,16,1280]{2,1,0:T(8,128)(2,1)S(1)}, u32[]{:S(2)}, u32[]{:S(2)}) collective-permute-start(bf16[4,16,1280]{2,1,0:T(8,128)(2,1)S(1)} %bitcast.46), channel_id=1, source_target_pairs={{0,2},{2,4},{4,6},{6,8},{8,10},{10,12},{12,14},{1,3},{3,5},{5,7},{... | collective-permute-start | bytes 491528 | tf_op jit(solution)/shard_map/ppermute | solution.py:15
  111.7 0.1 fusion.26
  111.8 1.8 %collective-permute-start.10 = (bf16[8,4]{1,0:T(8,128)(2,1)S(1)}, bf16[8,4]{1,0:T(8,128)(2,1)S(1)}, u32[]{:S(2)}, u32[]{:S(2)}) collective-permute-start(bf16[8,4]{1,0:T(8,128)(2,1)S(1)} %get-tuple-element.108), channel_id=1, source_target_pairs={{0,1},{2,3},{4,5},{6,7},{8,9},{10,11},{12,13},{14,15},{16,17},{18,... | collective-permute-start | bytes 200 | tf_op jit(solution)/shard_map/ppermute | solution.py:15
  113.6 1.3 collective-permute-start.11
  115.0 1.3 collective-permute-start.5
  116.3 0.0 collective-permute-done.4
  116.4 7.5 %collective-permute-done.5 = bf16[4,16,1280]{2,1,0:T(8,128)(2,1)S(1)} collective-permute-done((bf16[4,16,1280]{2,1,0:T(8,128)(2,1)S(1)}, bf16[4,16,1280]{2,1,0:T(8,128)(2,1)S(1)}, u32[]{:S(2)}, u32[]{:S(2)}) %collective-permute-start.5) | collective-permute-done | bytes 163872 | tf_op jit(solution)/shard_map/ppermute | solution.py:15
  123.8 0.1 fusion.14
  124.0 0.1 fusion.23
  124.0 2.0 %collective-permute-start.6 = (bf16[8,4,1280]{2,1,0:T(4,128)(2,1)S(1)}, bf16[8,4,1280]{2,1,0:T(4,128)(2,1)S(1)}, u32[]{:S(2)}, u32[]{:S(2)}) collective-permute-start(bf16[8,4,1280]{2,1,0:T(4,128)(2,1)S(1)} %get-tuple-element.100), channel_id=1, source_target_pairs={{0,1},{2,3},{4,5},{6,7},{8,9},{10,11},{12,13},{14,15},{16,17},{18,... | collective-permute-start | bytes 245768 | tf_op jit(solution)/shard_map/ppermute | solution.py:15
  126.1 1.3 collective-permute-start.7
  127.4 0.0 collective-permute-done.10
  127.4 0.0 collective-permute-done.11
  127.4 0.1 add_maximum_fusion
  127.5 0.0 collective-permute-done.6
  127.5 1.8 %collective-permute-done.7 = bf16[8,4,1280]{2,1,0:T(4,128)(2,1)S(1)} collective-permute-done((bf16[8,4,1280]{2,1,0:T(4,128)(2,1)S(1)}, bf16[8,4,1280]{2,1,0:T(4,128)(2,1)S(1)}, u32[]{:S(2)}, u32[]{:S(2)}) %collective-permute-start.7) | collective-permute-done | bytes 81952 | tf_op jit(solution)/shard_map/ppermute | solution.py:15
  129.2 0.8 fusion.13
  (17 shorter events, 0.2 us)
Async XLA Ops:
  6.5 59.8 %all-gather.3.cloned.1.call-start = ((), (), s32[]{:S(2)}) async-start(), calls=%async_computation | async-start | bytes 5222400 | tf_op jit(solution)/shard_map/all_gather | solution.py:106
  7.3 99.8 %all-gather.5.cloned.1.call-start = ((), (), s32[]{:S(2)}) async-start(), calls=%async_computation.1 | async-start | bytes 1740800 | tf_op jit(solution)/shard_map/all_gather | solution.py:115
  8.2 13.8 %collective-permute-start = (bf16[4,8,1280]{2,1,0:T(8,128)(2,1)S(1)}, bf16[4,8,1280]{2,1,0:T(8,128)(2,1)S(1)}, u32[]{:S(2)}, u32[]{:S(2)}) collective-permute-start(bf16[4,8,1280]{2,1,0:T(8,128)(2,1)S(1)} %get-tuple-element.105), channel_id=1, source_target_pairs={{0,2},{2,4},{4,6},{6,8},{8,10},{10,12},{12,14},{1,3},{3,5},{5,7},{... | collective-permute-start | bytes 245768 | tf_op jit(solution)/shard_map/ppermute | solution.py:23
  13.1 10.0 %collective-permute-start.1 = (bf16[4,8,1280]{2,1,0:T(8,128)(2,1)S(1)}, bf16[4,8,1280]{2,1,0:T(8,128)(2,1)S(1)}, u32[]{:S(2)}, u32[]{:S(2)}) collective-permute-start(bf16[4,8,1280]{2,1,0:T(8,128)(2,1)S(1)} %get-tuple-element.104), channel_id=1, source_target_pairs={{2,0},{4,2},{6,4},{8,6},{10,8},{12,10},{14,12},{3,1},{5,3},{7,5},{... | collective-permute-start | bytes 245768 | tf_op jit(solution)/shard_map/ppermute | solution.py:26
  15.3 6.7 %collective-permute-start.8 = (bf16[4,16]{1,0:T(4,128)(2,1)S(1)}, bf16[4,16]{1,0:T(4,128)(2,1)S(1)}, u32[]{:S(2)}, u32[]{:S(2)}) collective-permute-start(bf16[4,16]{1,0:T(4,128)(2,1)S(1)} %get-tuple-element.107), channel_id=1, source_target_pairs={{0,2},{2,4},{4,6},{6,8},{8,10},{10,12},{12,14},{1,3},{3,5},{5,7},{... | collective-permute-start | bytes 392 | tf_op jit(solution)/shard_map/ppermute | solution.py:15
  19.9 6.0 %collective-permute-start.9 = (bf16[4,16]{1,0:T(4,128)(2,1)S(1)}, bf16[4,16]{1,0:T(4,128)(2,1)S(1)}, u32[]{:S(2)}, u32[]{:S(2)}) collective-permute-start(bf16[4,16]{1,0:T(4,128)(2,1)S(1)} %get-tuple-element.106), channel_id=1, source_target_pairs={{2,0},{4,2},{6,4},{8,6},{10,8},{12,10},{14,12},{3,1},{5,3},{7,5},{... | collective-permute-start | bytes 392 | tf_op jit(solution)/shard_map/ppermute | solution.py:15
  22.1 6.1 %copy-start = (bf16[256,1280]{1,0:T(8,128)(2,1)S(1)}, bf16[256,1280]{1,0:T(8,128)(2,1)}, u32[]{:S(2)}) copy-start(bf16[256,1280]{1,0:T(8,128)(2,1)} %param.26) | copy-start | bytes 1966084
  23.2 2.7 %collective-permute-start.2 = (bf16[16,4,1280]{2,1,0:T(4,128)(2,1)S(1)}, bf16[16,4,1280]{2,1,0:T(4,128)(2,1)S(1)}, u32[]{:S(2)}, u32[]{:S(2)}) collective-permute-start(bf16[16,4,1280]{2,1,0:T(4,128)(2,1)S(1)} %get-tuple-element.102), channel_id=1, source_target_pairs={{0,1},{2,3},{4,5},{6,7},{8,9},{10,11},{12,13},{14,15},{16,17},{18,... | collective-permute-start | bytes 491528 | tf_op jit(solution)/shard_map/ppermute | solution.py:23
  24.6 3.3 %collective-permute-start.3 = (bf16[16,4,1280]{2,1,0:T(4,128)(2,1)S(1)}, bf16[16,4,1280]{2,1,0:T(4,128)(2,1)S(1)}, u32[]{:S(2)}, u32[]{:S(2)}) collective-permute-start(bf16[16,4,1280]{2,1,0:T(4,128)(2,1)S(1)} %get-tuple-element.103), channel_id=1, source_target_pairs={{1,0},{3,2},{5,4},{7,6},{9,8},{11,10},{13,12},{15,14},{17,16},{19,... | collective-permute-start | bytes 491528 | tf_op jit(solution)/shard_map/ppermute | solution.py:26
  28.2 38.2 %copy-start.2 = (f32[1920]{0:T(1024)S(1)}, f32[1920]{0:T(1024)}, u32[]{:S(2)}) copy-start(f32[1920]{0:T(1024)} %param.30) | copy-start | bytes 23044
  28.2 38.2 %copy-start.3 = (f32[1280]{0:T(1024)S(1)}, f32[1280]{0:T(1024)}, u32[]{:S(2)}) copy-start(f32[1280]{0:T(1024)} %param.28) | copy-start | bytes 15364
  28.2 38.2 %copy-start.4 = (f32[1280]{0:T(1024)S(1)}, f32[1280]{0:T(1024)}, u32[]{:S(2)}) copy-start(f32[1280]{0:T(1024)} %param.27) | copy-start | bytes 15364
  73.3 33.7 %copy-start.1 = (f32[1280]{0:T(1024)S(1)}, f32[1280]{0:T(1024)}, u32[]{:S(2)}) copy-start(f32[1280]{0:T(1024)} %param.32) | copy-start | bytes 15364
  109.3 7.0 %collective-permute-start.4 = (bf16[4,16,1280]{2,1,0:T(8,128)(2,1)S(1)}, bf16[4,16,1280]{2,1,0:T(8,128)(2,1)S(1)}, u32[]{:S(2)}, u32[]{:S(2)}) collective-permute-start(bf16[4,16,1280]{2,1,0:T(8,128)(2,1)S(1)} %bitcast.46), channel_id=1, source_target_pairs={{0,2},{2,4},{4,6},{6,8},{8,10},{10,12},{12,14},{1,3},{3,5},{5,7},{... | collective-permute-start | bytes 491528 | tf_op jit(solution)/shard_map/ppermute | solution.py:15
  111.8 15.6 %collective-permute-start.10 = (bf16[8,4]{1,0:T(8,128)(2,1)S(1)}, bf16[8,4]{1,0:T(8,128)(2,1)S(1)}, u32[]{:S(2)}, u32[]{:S(2)}) collective-permute-start(bf16[8,4]{1,0:T(8,128)(2,1)S(1)} %get-tuple-element.108), channel_id=1, source_target_pairs={{0,1},{2,3},{4,5},{6,7},{8,9},{10,11},{12,13},{14,15},{16,17},{18,... | collective-permute-start | bytes 200 | tf_op jit(solution)/shard_map/ppermute | solution.py:15
  113.6 13.7 %collective-permute-start.11 = (bf16[8,4]{1,0:T(8,128)(2,1)S(1)}, bf16[8,4]{1,0:T(8,128)(2,1)S(1)}, u32[]{:S(2)}, u32[]{:S(2)}) collective-permute-start(bf16[8,4]{1,0:T(8,128)(2,1)S(1)} %get-tuple-element.109), channel_id=1, source_target_pairs={{1,0},{3,2},{5,4},{7,6},{9,8},{11,10},{13,12},{15,14},{17,16},{19,... | collective-permute-start | bytes 200 | tf_op jit(solution)/shard_map/ppermute | solution.py:15
  115.0 8.8 %collective-permute-start.5 = (bf16[4,16,1280]{2,1,0:T(8,128)(2,1)S(1)}, bf16[4,16,1280]{2,1,0:T(8,128)(2,1)S(1)}, u32[]{:S(2)}, u32[]{:S(2)}) collective-permute-start(bf16[4,16,1280]{2,1,0:T(8,128)(2,1)S(1)} %bitcast.45), channel_id=1, source_target_pairs={{2,0},{4,2},{6,4},{8,6},{10,8},{12,10},{14,12},{3,1},{5,3},{7,5},{... | collective-permute-start | bytes 491528 | tf_op jit(solution)/shard_map/ppermute | solution.py:15
  124.0 3.4 %collective-permute-start.6 = (bf16[8,4,1280]{2,1,0:T(4,128)(2,1)S(1)}, bf16[8,4,1280]{2,1,0:T(4,128)(2,1)S(1)}, u32[]{:S(2)}, u32[]{:S(2)}) collective-permute-start(bf16[8,4,1280]{2,1,0:T(4,128)(2,1)S(1)} %get-tuple-element.100), channel_id=1, source_target_pairs={{0,1},{2,3},{4,5},{6,7},{8,9},{10,11},{12,13},{14,15},{16,17},{18,... | collective-permute-start | bytes 245768 | tf_op jit(solution)/shard_map/ppermute | solution.py:15
  126.1 3.2 %collective-permute-start.7 = (bf16[8,4,1280]{2,1,0:T(4,128)(2,1)S(1)}, bf16[8,4,1280]{2,1,0:T(4,128)(2,1)S(1)}, u32[]{:S(2)}, u32[]{:S(2)}) collective-permute-start(bf16[8,4,1280]{2,1,0:T(4,128)(2,1)S(1)} %get-tuple-element.101), channel_id=1, source_target_pairs={{1,0},{3,2},{5,4},{7,6},{9,8},{11,10},{13,12},{15,14},{17,16},{19,... | collective-permute-start | bytes 245768 | tf_op jit(solution)/shard_map/ppermute | solution.py:15
Sparse Core Ops, SparseCore 0:
  9.5 56.8 all-gather.2
  68.5 38.4 all-gather.4
where the time goes:
time: 137 us
  waiting for transfers between devices  81.2 us (59%)
  starting transfers between devices  24.7 us (18%)
  between operations  13.7 us (10%)
  matrix products  10.6 us (8%)
  other arithmetic  3.6 us (3%)
  local copies, waits for them, and re-layouts  3.12 us (2%)
    all_gather x1, waiting for transfers between devices, body(): lax.all_gather(w_qkv, ('row', 'col'), axis=0, tiled=True)  37.5 us
    all_gather x1, waiting for transfers between devices, body(): lax.all_gather(w_out, ('row', 'col'), axis=0, tiled=True)  31.7 us
    ppermute x8, starting transfers between devices, shifted(): lax.ppermute(value, axis, [(source, source + steps) for source in range(i...  15.9 us
    ppermute x8, waiting for transfers between devices, shifted(): lax.ppermute(value, axis, [(source, source + steps) for source in range(i...  9.3 us
    ppermute x2, starting transfers between devices, extended(): lax.ppermute(lax.slice_in_dim(block, block.shape[dim] - width, None, axis...  6.17 us
    dot_general x1, matrix products, body(): jnp.dot(normed, lax.all_gather(w_qkv, ('row', 'col'), axis=0, tiled=True)...  4.14 us
  transfers between devices with their start and end apart: 14, of which 6 were waited for; matrix products, arithmetic and copies ran while one was open for 10% of the time, Pallas kernels for 0%

commit v1 on v0

--- a/solution.py
+++ b/solution.py
@@ -1,3 +1,4 @@
+import functools
 import jax
 import jax.numpy as jnp
 from jax import lax
@@ -7,6 +8,32 @@
 EPSILON = 1e-06
 SPREAD = 4.0
 FLOOR = 0.25
+
+
+def _link_points(chunk, comm_axis):
+    piece_out = lax.axis_size(comm_axis)
+    tall = lax.axis_index(comm_axis)
+    state_next, prior, current_value = (piece_out, tall, chunk.shape[0])
+    next_value = tuple((k0 * state_next if m == 0 else k0 for m, k0 in enumerate(chunk.shape)))
+    carry_in = jnp.zeros(next_value, chunk.dtype)
+    big = lax.dynamic_update_slice_in_dim(carry_in, chunk, prior * current_value, axis=0)
+    a_now = piece_now = chunk
+    for t in range(1, state_next // 2 + 1):
+        formed = tuple(((m, (m + 1) % state_next) for m in range(state_next)))
+        a_now = lax.ppermute(a_now, comm_axis, formed)
+        big = lax.dynamic_update_slice_in_dim(
+            big, a_now, (prior - t) % state_next * current_value, axis=0
+        )
+        if 2 * t < state_next:
+            w2 = tuple(((m, (m - 1) % state_next) for m in range(state_next)))
+            piece_now = lax.ppermute(piece_now, comm_axis, w2)
+            big = lax.dynamic_update_slice_in_dim(
+                big, piece_now, (prior + t) % state_next * current_value, axis=0
+            )
+    return big
+
+
+list_keys_for = functools.partial(_link_points, comm_axis=("row", "col"))
 
 
 def shifted(value, axis, steps):
@@ -111,10 +138,7 @@
     )
     attended = jax.vmap(attend)(projected).reshape(tile_rows * rows_count, -1)
     projected_out = lax.dot_general(
-        attended,
-        lax.all_gather(w_out, ("row", "col"), axis=0, tiled=True),
-        (((1,), (1,)), ((), ())),
-        preferred_element_type=jnp.float32,
+        attended, list_keys_for(w_out), (((1,), (1,)), ((), ())), preferred_element_type=jnp.float32
     )
     hidden = inputs + projected_out + b_out
     gauss = gauss_table(win).reshape(1, rows_count)

time: 137 us -> 130 us (0.949)
  waiting for transfers between devices: 81.2 us -> 36.4 us
  starting transfers between devices: 24.7 us -> 57.4 us
  local copies, waits for them, and re-layouts: 3.12 us -> 7.55 us
    all_gather x1, waiting for transfers between devices: 37.5 us -> 0.02 us  [body(): lax.all_gather(w_qkv, ('row', 'col'), axis=0, tiled=True)]
    ppermute x0 -> x15, starting transfers between devices: none -> 33 us  [the longest x7 32.4 us: _link_points(): piece_now = lax.ppermute(piece_now, comm_axis, w2)]
    all_gather x1 -> x0, waiting for transfers between devices: 31.7 us -> none  [body(): lax.all_gather(w_out, ('row', 'col'), axis=0, tiled=True)]
    ppermute x0 -> x15, waiting for transfers between devices: none -> 23.7 us  [the longest x8 15.5 us: _link_points(): a_now = lax.ppermute(a_now, comm_axis, formed)]
    ppermute x8, waiting for transfers between devices: 9.3 us -> 11.9 us  [shifted(): lax.ppermute(value, axis, [(source, source + steps) for source in range(i...]
    ppermute x2, waiting for transfers between devices: 1.92 us -> 0.01 us  [extended(): lax.ppermute(lax.slice_in_dim(block, 0, width, axis=dim), axis, backward)]
    ppermute x2, starting transfers between devices: 6.17 us -> 4.34 us  [extended(): lax.ppermute(lax.slice_in_dim(block, block.shape[dim] - width, None, axis...]
    slice x1, local copies, waits for them, and re-layouts: 0.19 us -> 1.88 us  [attend(): queries = projected[:, :width].reshape(rows_count, HEADS, head_size)]
  transfers between devices with their start and end apart: 14 -> 28, of which waited for: 6 -> 16; matrix products, arithmetic and copies ran while one was open for 10% -> 4% of each run, Pallas kernels for 0% -> 0%
where the time goes in v1:
time: 130 us; the launch traced here: 129 us
  starting transfers between devices  57.4 us (44%)
  waiting for transfers between devices  36.4 us (28%)
  between operations  14.2 us (11%)
  matrix products  10.1 us (8%)
  local copies, waits for them, and re-layouts  7.55 us (6%)
  other arithmetic  3.53 us (3%)
    ppermute x7, starting transfers between devices, _link_points(): piece_now = lax.ppermute(piece_now, comm_axis, w2)  32.4 us
    ppermute x8, starting transfers between devices, shifted(): lax.ppermute(value, axis, [(source, source + steps) for source in range(i...  17.3 us
    ppermute x8, waiting for transfers between devices, _link_points(): a_now = lax.ppermute(a_now, comm_axis, formed)  15.5 us
    ppermute x8, waiting for transfers between devices, shifted(): lax.ppermute(value, axis, [(source, source + steps) for source in range(i...  11.9 us
    ppermute x7, waiting for transfers between devices, _link_points(): piece_now = lax.ppermute(piece_now, comm_axis, w2)  8.22 us
    ppermute x2, starting transfers between devices, extended(): lax.ppermute(lax.slice_in_dim(block, block.shape[dim] - width, None, axis...  4.34 us
    dot_general x1, matrix products, body(): jnp.dot(normed, lax.all_gather(w_qkv, ('row', 'col'), axis=0, tiled=True)...  4.1 us
    sub x1, matrix products, attend(): expon = jnp.exp(scores - highest)  3.31 us
  transfers between devices with their start and end apart: 28, of which 16 were waited for; matrix products, arithmetic and copies ran while one was open for 4% of the time, Pallas kernels for 0%

profile of v1, /device:TPU:0, one launch (start us, length us, event | category | flops | bytes accessed | tf_op | source)
XLA Modules:
  0.0 129.2 jit_solution(5375665522742085773)
XLA Ops:
  6.5 0.7 all-gather.2.cloned.1.call-update
  7.3 0.5 collective-permute-start.4
  7.8 5.0 %collective-permute-start.5 = (bf16[80,640]{1,0:T(8,128)(2,1)}, bf16[80,640]{1,0:T(8,128)(2,1)S(1)}, u32[]{:S(2)}, u32[]{:S(2)}) collective-permute-start(bf16[80,640]{1,0:T(8,128)(2,1)} %param.31), channel_id=1, source_target_pairs={{0,15},{1,0},{2,1},{3,2},{4,3},{5,4},{6,5},{7,6},{8,7},{9,8},{10,9... | collective-permute-start | bytes 307208 | tf_op jit(solution)/shard_map/ppermute | solution.py:29
  12.8 0.9 fusion.24
  13.8 1.3 %collective-permute-start = (bf16[4,8,1280]{2,1,0:T(8,128)(2,1)S(1)}, bf16[4,8,1280]{2,1,0:T(8,128)(2,1)S(1)}, u32[]{:S(2)}, u32[]{:S(2)}) collective-permute-start(bf16[4,8,1280]{2,1,0:T(8,128)(2,1)S(1)} %get-tuple-element.105), channel_id=1, source_target_pairs={{0,2},{2,4},{4,6},{6,8},{8,10},{10,12},{12,14},{1,3},{3,5},{5,7},{... | collective-permute-start | bytes 245768 | tf_op jit(solution)/shard_map/ppermute | solution.py:50
  15.1 1.3 %collective-permute-start.1 = (bf16[4,8,1280]{2,1,0:T(8,128)(2,1)S(1)}, bf16[4,8,1280]{2,1,0:T(8,128)(2,1)S(1)}, u32[]{:S(2)}, u32[]{:S(2)}) collective-permute-start(bf16[4,8,1280]{2,1,0:T(8,128)(2,1)S(1)} %get-tuple-element.104), channel_id=1, source_target_pairs={{2,0},{4,2},{6,4},{8,6},{10,8},{12,10},{14,12},{3,1},{5,3},{7,5},{... | collective-permute-start | bytes 245768 | tf_op jit(solution)/shard_map/ppermute | solution.py:53
  16.4 0.7 convert_reduce_fusion
  17.1 0.1 convert_element_type.105
  17.2 0.1 fusion.19
  17.3 4.8 %collective-permute-start.23 = (bf16[4,16]{1,0:T(4,128)(2,1)S(1)}, bf16[4,16]{1,0:T(4,128)(2,1)S(1)}, u32[]{:S(2)}, u32[]{:S(2)}) collective-permute-start(bf16[4,16]{1,0:T(4,128)(2,1)S(1)} %get-tuple-element.107), channel_id=1, source_target_pairs={{0,2},{2,4},{4,6},{6,8},{8,10},{10,12},{12,14},{1,3},{3,5},{5,7},{... | collective-permute-start | bytes 392 | tf_op jit(solution)/shard_map/ppermute | solution.py:42
  22.3 0.7 convert_element_type.90
  23.0 0.1 multiply_exponential_fusion
  23.1 0.1 exp.26
  23.2 0.1 broadcast_in_dim.2
  23.4 1.3 %collective-permute-start.24 = (bf16[4,16]{1,0:T(4,128)(2,1)S(1)}, bf16[4,16]{1,0:T(4,128)(2,1)S(1)}, u32[]{:S(2)}, u32[]{:S(2)}) collective-permute-start(bf16[4,16]{1,0:T(4,128)(2,1)S(1)} %get-tuple-element.106), channel_id=1, source_target_pairs={{2,0},{4,2},{6,4},{8,6},{10,8},{12,10},{14,12},{3,1},{5,3},{7,5},{... | collective-permute-start | bytes 392 | tf_op jit(solution)/shard_map/ppermute | solution.py:42
  24.7 5.1 %collective-permute-done.24 = bf16[4,16]{1,0:T(4,128)(2,1)S(1)} collective-permute-done((bf16[4,16]{1,0:T(4,128)(2,1)S(1)}, bf16[4,16]{1,0:T(4,128)(2,1)S(1)}, u32[]{:S(2)}, u32[]{:S(2)}) %collective-permute-start.24) | collective-permute-done | bytes 160 | tf_op jit(solution)/shard_map/ppermute | solution.py:42
  29.9 0.1 fusion.23
  30.0 1.4 %collective-permute-start.3 = (bf16[16,4,1280]{2,1,0:T(4,128)(2,1)S(1)}, bf16[16,4,1280]{2,1,0:T(4,128)(2,1)S(1)}, u32[]{:S(2)}, u32[]{:S(2)}) collective-permute-start(bf16[16,4,1280]{2,1,0:T(4,128)(2,1)S(1)} %get-tuple-element.103), channel_id=1, source_target_pairs={{1,0},{3,2},{5,4},{7,6},{9,8},{11,10},{13,12},{15,14},{17,16},{19,... | collective-permute-start | bytes 491528 | tf_op jit(solution)/shard_map/ppermute | solution.py:53
  31.4 3.0 %collective-permute-start.2 = (bf16[16,4,1280]{2,1,0:T(4,128)(2,1)S(1)}, bf16[16,4,1280]{2,1,0:T(4,128)(2,1)S(1)}, u32[]{:S(2)}, u32[]{:S(2)}) collective-permute-start(bf16[16,4,1280]{2,1,0:T(4,128)(2,1)S(1)} %get-tuple-element.102), channel_id=1, source_target_pairs={{0,1},{2,3},{4,5},{6,7},{8,9},{10,11},{12,13},{14,15},{16,17},{18,... | collective-permute-start | bytes 491528 | tf_op jit(solution)/shard_map/ppermute | solution.py:50
  34.5 0.1 collective-permute-start.6
  34.6 4.4 %collective-permute-start.7 = (bf16[80,640]{1,0:T(8,128)(2,1)S(1)}, bf16[80,640]{1,0:T(8,128)(2,1)S(1)}, u32[]{:S(2)}, u32[]{:S(2)}) collective-permute-start(bf16[80,640]{1,0:T(8,128)(2,1)S(1)} %collective-permute-done.5), channel_id=1, source_target_pairs={{0,15},{1,0},{2,1},{3,2},{4,3},{5,4},{6,5},{7,6},{8,7},{9,8},{10,9... | collective-permute-start | bytes 307208 | tf_op jit(solution)/shard_map/ppermute | solution.py:29
  39.0 2.3 %collective-permute-done.6 = bf16[80,640]{1,0:T(8,128)(2,1)S(1)} collective-permute-done((bf16[80,640]{1,0:T(8,128)(2,1)S(1)}, bf16[80,640]{1,0:T(8,128)(2,1)S(1)}, u32[]{:S(2)}, u32[]{:S(2)}) %collective-permute-start.6) | collective-permute-done | bytes 102432 | tf_op jit(solution)/shard_map/ppermute | solution.py:23
  41.4 1.8 %collective-permute-done.7 = bf16[80,640]{1,0:T(8,128)(2,1)S(1)} collective-permute-done((bf16[80,640]{1,0:T(8,128)(2,1)S(1)}, bf16[80,640]{1,0:T(8,128)(2,1)S(1)}, u32[]{:S(2)}, u32[]{:S(2)}) %collective-permute-start.7) | collective-permute-done | bytes 102432 | tf_op jit(solution)/shard_map/ppermute | solution.py:29
  43.2 4.6 %collective-permute-start.9 = (bf16[80,640]{1,0:T(8,128)(2,1)S(1)}, bf16[80,640]{1,0:T(8,128)(2,1)S(1)}, u32[]{:S(2)}, u32[]{:S(2)}) collective-permute-start(bf16[80,640]{1,0:T(8,128)(2,1)S(1)} %collective-permute-done.7), channel_id=1, source_target_pairs={{0,15},{1,0},{2,1},{3,2},{4,3},{5,4},{6,5},{7,6},{8,7},{9,8},{10,9... | collective-permute-start | bytes 307208 | tf_op jit(solution)/shard_map/ppermute | solution.py:29
  47.9 0.3 pad_maximum_fusion
  48.2 0.3 fusion.6
  48.5 0.3 multiply_reduce_fusion.1
  48.9 1.6 %collective-permute-done.8 = bf16[80,640]{1,0:T(8,128)(2,1)S(1)} collective-permute-done((bf16[80,640]{1,0:T(8,128)(2,1)S(1)}, bf16[80,640]{1,0:T(8,128)(2,1)S(1)}, u32[]{:S(2)}, u32[]{:S(2)}) %collective-permute-start.8) | collective-permute-done | bytes 102432 | tf_op jit(solution)/shard_map/ppermute | solution.py:23
  50.5 1.4 %collective-permute-done.9 = bf16[80,640]{1,0:T(8,128)(2,1)S(1)} collective-permute-done((bf16[80,640]{1,0:T(8,128)(2,1)S(1)}, bf16[80,640]{1,0:T(8,128)(2,1)S(1)}, u32[]{:S(2)}, u32[]{:S(2)}) %collective-permute-start.9) | collective-permute-done | bytes 102432 | tf_op jit(solution)/shard_map/ppermute | solution.py:29
  51.9 4.6 %collective-permute-start.11 = (bf16[80,640]{1,0:T(8,128)(2,1)S(1)}, bf16[80,640]{1,0:T(8,128)(2,1)S(1)}, u32[]{:S(2)}, u32[]{:S(2)}) collective-permute-start(bf16[80,640]{1,0:T(8,128)(2,1)S(1)} %collective-permute-done.9), channel_id=1, source_target_pairs={{0,15},{1,0},{2,1},{3,2},{4,3},{5,4},{6,5},{7,6},{8,7},{9,8},{10,9... | collective-permute-start | bytes 307208 | tf_op jit(solution)/shard_map/ppermute | solution.py:29
  56.5 1.8 %collective-permute-done.10 = bf16[80,640]{1,0:T(8,128)(2,1)S(1)} collective-permute-done((bf16[80,640]{1,0:T(8,128)(2,1)S(1)}, bf16[80,640]{1,0:T(8,128)(2,1)S(1)}, u32[]{:S(2)}, u32[]{:S(2)}) %collective-permute-start.10) | collective-permute-done | bytes 102432 | tf_op jit(solution)/shard_map/ppermute | solution.py:23
  58.4 0.4 collective-permute-done.11
  58.7 4.6 %collective-permute-start.13 = (bf16[80,640]{1,0:T(8,128)(2,1)S(1)}, bf16[80,640]{1,0:T(8,128)(2,1)S(1)}, u32[]{:S(2)}, u32[]{:S(2)}) collective-permute-start(bf16[80,640]{1,0:T(8,128)(2,1)S(1)} %collective-permute-done.11), channel_id=1, source_target_pairs={{0,15},{1,0},{2,1},{3,2},{4,3},{5,4},{6,5},{7,6},{8,7},{9,8},{10,9... | collective-permute-start | bytes 307208 | tf_op jit(solution)/shard_map/ppermute | solution.py:29
  63.4 1.9 %collective-permute-done.12 = bf16[80,640]{1,0:T(8,128)(2,1)S(1)} collective-permute-done((bf16[80,640]{1,0:T(8,128)(2,1)S(1)}, bf16[80,640]{1,0:T(8,128)(2,1)S(1)}, u32[]{:S(2)}, u32[]{:S(2)}) %collective-permute-start.12) | collective-permute-done | bytes 102432 | tf_op jit(solution)/shard_map/ppermute | solution.py:23
  65.4 2.4 %collective-permute-done.13 = bf16[80,640]{1,0:T(8,128)(2,1)S(1)} collective-permute-done((bf16[80,640]{1,0:T(8,128)(2,1)S(1)}, bf16[80,640]{1,0:T(8,128)(2,1)S(1)}, u32[]{:S(2)}, u32[]{:S(2)}) %collective-permute-start.13) | collective-permute-done | bytes 102432 | tf_op jit(solution)/shard_map/ppermute | solution.py:29
  67.8 4.6 %collective-permute-start.15 = (bf16[80,640]{1,0:T(8,128)(2,1)S(1)}, bf16[80,640]{1,0:T(8,128)(2,1)S(1)}, u32[]{:S(2)}, u32[]{:S(2)}) collective-permute-start(bf16[80,640]{1,0:T(8,128)(2,1)S(1)} %collective-permute-done.13), channel_id=1, source_target_pairs={{0,15},{1,0},{2,1},{3,2},{4,3},{5,4},{6,5},{7,6},{8,7},{9,8},{10,9... | collective-permute-start | bytes 307208 | tf_op jit(solution)/shard_map/ppermute | solution.py:29
  72.4 1.1 collective-permute-done.14
  73.5 1.1 collective-permute-done.15
  74.6 4.5 %collective-permute-start.17 = (bf16[80,640]{1,0:T(8,128)(2,1)S(1)}, bf16[80,640]{1,0:T(8,128)(2,1)S(1)}, u32[]{:S(2)}, u32[]{:S(2)}) collective-permute-start(bf16[80,640]{1,0:T(8,128)(2,1)S(1)} %collective-permute-done.15), channel_id=1, source_target_pairs={{0,15},{1,0},{2,1},{3,2},{4,3},{5,4},{6,5},{7,6},{8,7},{9,8},{10,9... | collective-permute-start | bytes 307208 | tf_op jit(solution)/shard_map/ppermute | solution.py:29
  79.2 1.1 collective-permute-done.16
  80.3 1.1 collective-permute-done.17
  81.5 5.6 %collective-permute-done.18 = bf16[80,640]{1,0:T(8,128)(2,1)S(1)} collective-permute-done((bf16[80,640]{1,0:T(8,128)(2,1)S(1)}, bf16[80,640]{1,0:T(8,128)(2,1)S(1)}, u32[]{:S(2)}, u32[]{:S(2)}) %collective-permute-start.18) | collective-permute-done | bytes 102432 | tf_op jit(solution)/shard_map/ppermute | solution.py:23
  87.1 0.0 all-gather.2.cloned.1.call-done
  87.1 4.1 %fusion.4 = bf16[1,256,1920]{2,1,0:T(8,128)(2,1)S(1)} fusion(bf16[1280,1920]{1,0:T(8,128)(2,1)} %all-gather.2.cloned.1.call-done, f32[1920]{0:T(1024)S(1)} %copy-done.5, bf16[256,1280]{1,0:T(8,128)(2,1)S(1)} %copy-done, bf16[256,1280]{1,0:T(8,128)(2,1)S(1)} %bitcast.37, f32[1280]{0:T(1024)S(1)} %copy-done.6, f32[1280]{0:T(1024)S(1)} %copy-done.7, ...), kind=kOutput, calls=%fused_computation.6 | convolution fusion | flops 1261895680 | bytes 7228928 | tf_op jit(solution)/shard_map/dot_general | solution.py:131
  91.2 0.9 fusion.20
  92.2 1.9 %copy.14 = bf16[1,256,640]{1,2,0:T(8,128)(2,1)} copy(bf16[1,256,640]{2,1,0:T(8,128)(2,1)} %get-tuple-element.97) | data formatting | bytes 655360 | tf_op jit(solution)/shard_map/vmap()/slice | solution.py:76
  94.0 1.9 %copy.15 = bf16[1,256,640]{1,2,0:T(8,128)(2,1)} copy(bf16[1,256,640]{2,1,0:T(8,128)(2,1)} %get-tuple-element.96) | data formatting | bytes 655360 | tf_op jit(solution)/shard_map/vmap()/slice | solution.py:74
  95.9 0.9 copy.16
  96.8 3.3 %fusion.26 = (f32[8,256]{1,0:T(8,128)S(1)}, f32[8,256,256]{1,2,0:T(8,128)}) fusion(bf16[256,8,80]{0,2,1:T(8,128)(2,1)} %bitcast.43, bf16[256,8,80]{0,2,1:T(8,128)(2,1)} %bitcast.44), kind=kOutput, calls=%fused_computation.71 | convolution fusion | flops 85459200 | bytes 2760704 | tf_op jit(solution)/shard_map/vmap()/sub | solution.py:81
  100.1 1.9 %convolution_convert_fusion = bf16[8,80,256]{2,1,0:T(8,128)(2,1)S(1)} fusion(bf16[256,8,80]{0,2,1:T(8,128)(2,1)S(1)} %bitcast.42, f32[8,256,256]{1,2,0:T(8,128)} %get-tuple-element.111, f32[8,256]{1,0:T(8,128)S(1)} %get-tuple-element.110), kind=kOutput, calls=%fused_computation.14 | convolution fusion | flops 85098496 | bytes 2760704 | tf_op jit(solution)/shard_map/vmap(hqk,khd->qhd)/dot_general | solution.py:83
  102.1 0.8 fusion.27
  102.9 1.3 %collective-permute-start.19 = (bf16[4,16,1280]{2,1,0:T(8,128)(2,1)S(1)}, bf16[4,16,1280]{2,1,0:T(8,128)(2,1)S(1)}, u32[]{:S(2)}, u32[]{:S(2)}) collective-permute-start(bf16[4,16,1280]{2,1,0:T(8,128)(2,1)S(1)} %bitcast.46), channel_id=1, source_target_pairs={{0,2},{2,4},{4,6},{6,8},{8,10},{10,12},{12,14},{1,3},{3,5},{5,7},{... | collective-permute-start | bytes 491528 | tf_op jit(solution)/shard_map/ppermute | solution.py:42
  104.2 0.1 fusion.25
  104.3 1.3 collective-permute-start.26
  105.6 3.0 %collective-permute-start.25 = (bf16[8,4]{1,0:T(8,128)(2,1)S(1)}, bf16[8,4]{1,0:T(8,128)(2,1)S(1)}, u32[]{:S(2)}, u32[]{:S(2)}) collective-permute-start(bf16[8,4]{1,0:T(8,128)(2,1)S(1)} %get-tuple-element.108), channel_id=1, source_target_pairs={{0,1},{2,3},{4,5},{6,7},{8,9},{10,11},{12,13},{14,15},{16,17},{18,... | collective-permute-start | bytes 200 | tf_op jit(solution)/shard_map/ppermute | solution.py:42
  108.7 1.3 %collective-permute-start.20 = (bf16[4,16,1280]{2,1,0:T(8,128)(2,1)S(1)}, bf16[4,16,1280]{2,1,0:T(8,128)(2,1)S(1)}, u32[]{:S(2)}, u32[]{:S(2)}) collective-permute-start(bf16[4,16,1280]{2,1,0:T(8,128)(2,1)S(1)} %bitcast.45), channel_id=1, source_target_pairs={{2,0},{4,2},{6,4},{8,6},{10,8},{12,10},{14,12},{3,1},{5,3},{7,5},{... | collective-permute-start | bytes 491528 | tf_op jit(solution)/shard_map/ppermute | solution.py:42
  110.1 6.0 %collective-permute-done.20 = bf16[4,16,1280]{2,1,0:T(8,128)(2,1)S(1)} collective-permute-done((bf16[4,16,1280]{2,1,0:T(8,128)(2,1)S(1)}, bf16[4,16,1280]{2,1,0:T(8,128)(2,1)S(1)}, u32[]{:S(2)}, u32[]{:S(2)}) %collective-permute-start.20) | collective-permute-done | bytes 163872 | tf_op jit(solution)/shard_map/ppermute | solution.py:42
  116.1 0.1 fusion.14
  116.2 0.1 fusion.22
  116.3 1.3 %collective-permute-start.22 = (bf16[8,4,1280]{2,1,0:T(4,128)(2,1)S(1)}, bf16[8,4,1280]{2,1,0:T(4,128)(2,1)S(1)}, u32[]{:S(2)}, u32[]{:S(2)}) collective-permute-start(bf16[8,4,1280]{2,1,0:T(4,128)(2,1)S(1)} %get-tuple-element.101), channel_id=1, source_target_pairs={{1,0},{3,2},{5,4},{7,6},{9,8},{11,10},{13,12},{15,14},{17,16},{19,... | collective-permute-start | bytes 245768 | tf_op jit(solution)/shard_map/ppermute | solution.py:42
  117.6 3.0 %collective-permute-start.21 = (bf16[8,4,1280]{2,1,0:T(4,128)(2,1)S(1)}, bf16[8,4,1280]{2,1,0:T(4,128)(2,1)S(1)}, u32[]{:S(2)}, u32[]{:S(2)}) collective-permute-start(bf16[8,4,1280]{2,1,0:T(4,128)(2,1)S(1)} %get-tuple-element.100), channel_id=1, source_target_pairs={{0,1},{2,3},{4,5},{6,7},{8,9},{10,11},{12,13},{14,15},{16,17},{18,... | collective-permute-start | bytes 245768 | tf_op jit(solution)/shard_map/ppermute | solution.py:42
  120.7 0.1 add_maximum_fusion
  120.7 0.8 collective-permute-done.21
  121.5 0.8 fusion.13
  (67 shorter events, 0.7 us)
Async XLA Ops:
  6.5 16.8 %copy-start.3 = (bf16[80,640]{1,0:T(8,128)(2,1)S(1)}, bf16[80,640]{1,0:T(8,128)(2,1)}, u32[]{:S(2)}) copy-start(bf16[80,640]{1,0:T(8,128)(2,1)} %param.31) | copy-start | bytes 307204
  6.5 23.3 %copy-start.1 = (bf16[8,8,1280]{2,1,0:T(8,128)(2,1)S(1)}, bf16[8,8,1280]{2,1,0:T(8,128)(2,1)}, u32[]{:S(2)}) copy-start(bf16[8,8,1280]{2,1,0:T(8,128)(2,1)} %param.25) | copy-start | bytes 491524
  6.5 80.6 %all-gather.2.cloned.1.call-start = ((), (), s32[]{:S(2)}) async-start(), calls=%async_computation | async-start | bytes 5222400 | tf_op jit(solution)/shard_map/all_gather | solution.py:133
  7.3 27.2 %collective-permute-start.4 = (bf16[80,640]{1,0:T(8,128)(2,1)}, bf16[80,640]{1,0:T(8,128)(2,1)S(1)}, u32[]{:S(2)}, u32[]{:S(2)}) collective-permute-start(bf16[80,640]{1,0:T(8,128)(2,1)} %param.31), channel_id=1, source_target_pairs={{0,1},{1,2},{2,3},{3,4},{4,5},{5,6},{6,7},{7,8},{8,9},{9,10},{10,1... | collective-permute-start | bytes 307208 | tf_op jit(solution)/shard_map/ppermute | solution.py:23
  7.8 26.8 %collective-permute-start.5 = (bf16[80,640]{1,0:T(8,128)(2,1)}, bf16[80,640]{1,0:T(8,128)(2,1)S(1)}, u32[]{:S(2)}, u32[]{:S(2)}) collective-permute-start(bf16[80,640]{1,0:T(8,128)(2,1)} %param.31), channel_id=1, source_target_pairs={{0,15},{1,0},{2,1},{3,2},{4,3},{5,4},{6,5},{7,6},{8,7},{9,8},{10,9... | collective-permute-start | bytes 307208 | tf_op jit(solution)/shard_map/ppermute | solution.py:29
  13.8 16.0 %collective-permute-start = (bf16[4,8,1280]{2,1,0:T(8,128)(2,1)S(1)}, bf16[4,8,1280]{2,1,0:T(8,128)(2,1)S(1)}, u32[]{:S(2)}, u32[]{:S(2)}) collective-permute-start(bf16[4,8,1280]{2,1,0:T(8,128)(2,1)S(1)} %get-tuple-element.105), channel_id=1, source_target_pairs={{0,2},{2,4},{4,6},{6,8},{8,10},{10,12},{12,14},{1,3},{3,5},{5,7},{... | collective-permute-start | bytes 245768 | tf_op jit(solution)/shard_map/ppermute | solution.py:50
  15.1 14.8 %collective-permute-start.1 = (bf16[4,8,1280]{2,1,0:T(8,128)(2,1)S(1)}, bf16[4,8,1280]{2,1,0:T(8,128)(2,1)S(1)}, u32[]{:S(2)}, u32[]{:S(2)}) collective-permute-start(bf16[4,8,1280]{2,1,0:T(8,128)(2,1)S(1)} %get-tuple-element.104), channel_id=1, source_target_pairs={{2,0},{4,2},{6,4},{8,6},{10,8},{12,10},{14,12},{3,1},{5,3},{7,5},{... | collective-permute-start | bytes 245768 | tf_op jit(solution)/shard_map/ppermute | solution.py:53
  17.3 6.1 %collective-permute-start.23 = (bf16[4,16]{1,0:T(4,128)(2,1)S(1)}, bf16[4,16]{1,0:T(4,128)(2,1)S(1)}, u32[]{:S(2)}, u32[]{:S(2)}) collective-permute-start(bf16[4,16]{1,0:T(4,128)(2,1)S(1)} %get-tuple-element.107), channel_id=1, source_target_pairs={{0,2},{2,4},{4,6},{6,8},{8,10},{10,12},{12,14},{1,3},{3,5},{5,7},{... | collective-permute-start | bytes 392 | tf_op jit(solution)/shard_map/ppermute | solution.py:42
  23.4 6.4 %collective-permute-start.24 = (bf16[4,16]{1,0:T(4,128)(2,1)S(1)}, bf16[4,16]{1,0:T(4,128)(2,1)S(1)}, u32[]{:S(2)}, u32[]{:S(2)}) collective-permute-start(bf16[4,16]{1,0:T(4,128)(2,1)S(1)} %get-tuple-element.106), channel_id=1, source_target_pairs={{2,0},{4,2},{6,4},{8,6},{10,8},{12,10},{14,12},{3,1},{5,3},{7,5},{... | collective-permute-start | bytes 392 | tf_op jit(solution)/shard_map/ppermute | solution.py:42
  29.8 18.4 %copy-start = (bf16[256,1280]{1,0:T(8,128)(2,1)S(1)}, bf16[256,1280]{1,0:T(8,128)(2,1)}, u32[]{:S(2)}) copy-start(bf16[256,1280]{1,0:T(8,128)(2,1)} %param.26) | copy-start | bytes 1966084
  30.0 17.8 %collective-permute-start.3 = (bf16[16,4,1280]{2,1,0:T(4,128)(2,1)S(1)}, bf16[16,4,1280]{2,1,0:T(4,128)(2,1)S(1)}, u32[]{:S(2)}, u32[]{:S(2)}) collective-permute-start(bf16[16,4,1280]{2,1,0:T(4,128)(2,1)S(1)} %get-tuple-element.103), channel_id=1, source_target_pairs={{1,0},{3,2},{5,4},{7,6},{9,8},{11,10},{13,12},{15,14},{17,16},{19,... | collective-permute-start | bytes 491528 | tf_op jit(solution)/shard_map/ppermute | solution.py:53
  31.4 16.4 %collective-permute-start.2 = (bf16[16,4,1280]{2,1,0:T(4,128)(2,1)S(1)}, bf16[16,4,1280]{2,1,0:T(4,128)(2,1)S(1)}, u32[]{:S(2)}, u32[]{:S(2)}) collective-permute-start(bf16[16,4,1280]{2,1,0:T(4,128)(2,1)S(1)} %get-tuple-element.102), channel_id=1, source_target_pairs={{0,1},{2,3},{4,5},{6,7},{8,9},{10,11},{12,13},{14,15},{16,17},{18,... | collective-permute-start | bytes 491528 | tf_op jit(solution)/shard_map/ppermute | solution.py:50
  34.5 6.9 %collective-permute-start.6 = (bf16[80,640]{1,0:T(8,128)(2,1)S(1)}, bf16[80,640]{1,0:T(8,128)(2,1)S(1)}, u32[]{:S(2)}, u32[]{:S(2)}) collective-permute-start(bf16[80,640]{1,0:T(8,128)(2,1)S(1)} %collective-permute-done.4), channel_id=1, source_target_pairs={{0,1},{1,2},{2,3},{3,4},{4,5},{5,6},{6,7},{7,8},{8,9},{9,10},{10,1... | collective-permute-start | bytes 307208 | tf_op jit(solution)/shard_map/ppermute | solution.py:23
  34.6 8.6 %collective-permute-start.7 = (bf16[80,640]{1,0:T(8,128)(2,1)S(1)}, bf16[80,640]{1,0:T(8,128)(2,1)S(1)}, u32[]{:S(2)}, u32[]{:S(2)}) collective-permute-start(bf16[80,640]{1,0:T(8,128)(2,1)S(1)} %collective-permute-done.5), channel_id=1, source_target_pairs={{0,15},{1,0},{2,1},{3,2},{4,3},{5,4},{6,5},{7,6},{8,7},{9,8},{10,9... | collective-permute-start | bytes 307208 | tf_op jit(solution)/shard_map/ppermute | solution.py:29
  41.4 9.1 %collective-permute-start.8 = (bf16[80,640]{1,0:T(8,128)(2,1)S(1)}, bf16[80,640]{1,0:T(8,128)(2,1)S(1)}, u32[]{:S(2)}, u32[]{:S(2)}) collective-permute-start(bf16[80,640]{1,0:T(8,128)(2,1)S(1)} %collective-permute-done.6), channel_id=1, source_target_pairs={{0,1},{1,2},{2,3},{3,4},{4,5},{5,6},{6,7},{7,8},{8,9},{9,10},{10,1... | collective-permute-start | bytes 307208 | tf_op jit(solution)/shard_map/ppermute | solution.py:23
  43.2 8.7 %collective-permute-start.9 = (bf16[80,640]{1,0:T(8,128)(2,1)S(1)}, bf16[80,640]{1,0:T(8,128)(2,1)S(1)}, u32[]{:S(2)}, u32[]{:S(2)}) collective-permute-start(bf16[80,640]{1,0:T(8,128)(2,1)S(1)} %collective-permute-done.7), channel_id=1, source_target_pairs={{0,15},{1,0},{2,1},{3,2},{4,3},{5,4},{6,5},{7,6},{8,7},{9,8},{10,9... | collective-permute-start | bytes 307208 | tf_op jit(solution)/shard_map/ppermute | solution.py:29
  48.5 38.7 %copy-start.5 = (f32[1920]{0:T(1024)S(1)}, f32[1920]{0:T(1024)}, u32[]{:S(2)}) copy-start(f32[1920]{0:T(1024)} %param.30) | copy-start | bytes 23044
  48.5 38.7 %copy-start.6 = (f32[1280]{0:T(1024)S(1)}, f32[1280]{0:T(1024)}, u32[]{:S(2)}) copy-start(f32[1280]{0:T(1024)} %param.28) | copy-start | bytes 15364
  48.5 38.7 %copy-start.7 = (f32[1280]{0:T(1024)S(1)}, f32[1280]{0:T(1024)}, u32[]{:S(2)}) copy-start(f32[1280]{0:T(1024)} %param.27) | copy-start | bytes 15364
  50.5 7.9 %collective-permute-start.10 = (bf16[80,640]{1,0:T(8,128)(2,1)S(1)}, bf16[80,640]{1,0:T(8,128)(2,1)S(1)}, u32[]{:S(2)}, u32[]{:S(2)}) collective-permute-start(bf16[80,640]{1,0:T(8,128)(2,1)S(1)} %collective-permute-done.8), channel_id=1, source_target_pairs={{0,1},{1,2},{2,3},{3,4},{4,5},{5,6},{6,7},{7,8},{8,9},{9,10},{10,1... | collective-permute-start | bytes 307208 | tf_op jit(solution)/shard_map/ppermute | solution.py:23
  51.9 6.9 %collective-permute-start.11 = (bf16[80,640]{1,0:T(8,128)(2,1)S(1)}, bf16[80,640]{1,0:T(8,128)(2,1)S(1)}, u32[]{:S(2)}, u32[]{:S(2)}) collective-permute-start(bf16[80,640]{1,0:T(8,128)(2,1)S(1)} %collective-permute-done.9), channel_id=1, source_target_pairs={{0,15},{1,0},{2,1},{3,2},{4,3},{5,4},{6,5},{7,6},{8,7},{9,8},{10,9... | collective-permute-start | bytes 307208 | tf_op jit(solution)/shard_map/ppermute | solution.py:29
  58.4 7.0 %collective-permute-start.12 = (bf16[80,640]{1,0:T(8,128)(2,1)S(1)}, bf16[80,640]{1,0:T(8,128)(2,1)S(1)}, u32[]{:S(2)}, u32[]{:S(2)}) collective-permute-start(bf16[80,640]{1,0:T(8,128)(2,1)S(1)} %collective-permute-done.10), channel_id=1, source_target_pairs={{0,1},{1,2},{2,3},{3,4},{4,5},{5,6},{6,7},{7,8},{8,9},{9,10},{10,1... | collective-permute-start | bytes 307208 | tf_op jit(solution)/shard_map/ppermute | solution.py:23
  58.7 9.1 %collective-permute-start.13 = (bf16[80,640]{1,0:T(8,128)(2,1)S(1)}, bf16[80,640]{1,0:T(8,128)(2,1)S(1)}, u32[]{:S(2)}, u32[]{:S(2)}) collective-permute-start(bf16[80,640]{1,0:T(8,128)(2,1)S(1)} %collective-permute-done.11), channel_id=1, source_target_pairs={{0,15},{1,0},{2,1},{3,2},{4,3},{5,4},{6,5},{7,6},{8,7},{9,8},{10,9... | collective-permute-start | bytes 307208 | tf_op jit(solution)/shard_map/ppermute | solution.py:29
  65.3 8.2 %collective-permute-start.14 = (bf16[80,640]{1,0:T(8,128)(2,1)S(1)}, bf16[80,640]{1,0:T(8,128)(2,1)S(1)}, u32[]{:S(2)}, u32[]{:S(2)}) collective-permute-start(bf16[80,640]{1,0:T(8,128)(2,1)S(1)} %collective-permute-done.12), channel_id=1, source_target_pairs={{0,1},{1,2},{2,3},{3,4},{4,5},{5,6},{6,7},{7,8},{8,9},{9,10},{10,1... | collective-permute-start | bytes 307208 | tf_op jit(solution)/shard_map/ppermute | solution.py:23
  67.8 6.9 %collective-permute-start.15 = (bf16[80,640]{1,0:T(8,128)(2,1)S(1)}, bf16[80,640]{1,0:T(8,128)(2,1)S(1)}, u32[]{:S(2)}, u32[]{:S(2)}) collective-permute-start(bf16[80,640]{1,0:T(8,128)(2,1)S(1)} %collective-permute-done.13), channel_id=1, source_target_pairs={{0,15},{1,0},{2,1},{3,2},{4,3},{5,4},{6,5},{7,6},{8,7},{9,8},{10,9... | collective-permute-start | bytes 307208 | tf_op jit(solution)/shard_map/ppermute | solution.py:29
  73.5 6.8 %collective-permute-start.16 = (bf16[80,640]{1,0:T(8,128)(2,1)S(1)}, bf16[80,640]{1,0:T(8,128)(2,1)S(1)}, u32[]{:S(2)}, u32[]{:S(2)}) collective-permute-start(bf16[80,640]{1,0:T(8,128)(2,1)S(1)} %collective-permute-done.14), channel_id=1, source_target_pairs={{0,1},{1,2},{2,3},{3,4},{4,5},{5,6},{6,7},{7,8},{8,9},{9,10},{10,1... | collective-permute-start | bytes 307208 | tf_op jit(solution)/shard_map/ppermute | solution.py:23
  74.6 6.8 %collective-permute-start.17 = (bf16[80,640]{1,0:T(8,128)(2,1)S(1)}, bf16[80,640]{1,0:T(8,128)(2,1)S(1)}, u32[]{:S(2)}, u32[]{:S(2)}) collective-permute-start(bf16[80,640]{1,0:T(8,128)(2,1)S(1)} %collective-permute-done.15), channel_id=1, source_target_pairs={{0,15},{1,0},{2,1},{3,2},{4,3},{5,4},{6,5},{7,6},{8,7},{9,8},{10,9... | collective-permute-start | bytes 307208 | tf_op jit(solution)/shard_map/ppermute | solution.py:29
  80.3 6.8 %collective-permute-start.18 = (bf16[80,640]{1,0:T(8,128)(2,1)S(1)}, bf16[80,640]{1,0:T(8,128)(2,1)S(1)}, u32[]{:S(2)}, u32[]{:S(2)}) collective-permute-start(bf16[80,640]{1,0:T(8,128)(2,1)S(1)} %collective-permute-done.16), channel_id=1, source_target_pairs={{0,1},{1,2},{2,3},{3,4},{4,5},{5,6},{6,7},{7,8},{8,9},{9,10},{10,1... | collective-permute-start | bytes 307208 | tf_op jit(solution)/shard_map/ppermute | solution.py:23
  96.8 3.3 %copy-start.2 = (bf16[1,256,640]{1,2,0:T(8,128)(2,1)S(1)}, bf16[1,256,640]{1,2,0:T(8,128)(2,1)}, u32[]{:S(2)}) copy-start(bf16[1,256,640]{1,2,0:T(8,128)(2,1)} %copy.14) | copy-start | bytes 983044
  100.1 1.9 %copy-start.4 = (f32[1280]{0:T(1024)S(1)}, f32[1280]{0:T(1024)}, u32[]{:S(2)}) copy-start(f32[1280]{0:T(1024)} %param.32) | copy-start | bytes 15364
  102.9 7.1 %collective-permute-start.19 = (bf16[4,16,1280]{2,1,0:T(8,128)(2,1)S(1)}, bf16[4,16,1280]{2,1,0:T(8,128)(2,1)S(1)}, u32[]{:S(2)}, u32[]{:S(2)}) collective-permute-start(bf16[4,16,1280]{2,1,0:T(8,128)(2,1)S(1)} %bitcast.46), channel_id=1, source_target_pairs={{0,2},{2,4},{4,6},{6,8},{8,10},{10,12},{12,14},{1,3},{3,5},{5,7},{... | collective-permute-start | bytes 491528 | tf_op jit(solution)/shard_map/ppermute | solution.py:42
  104.3 16.3 %collective-permute-start.26 = (bf16[8,4]{1,0:T(8,128)(2,1)S(1)}, bf16[8,4]{1,0:T(8,128)(2,1)S(1)}, u32[]{:S(2)}, u32[]{:S(2)}) collective-permute-start(bf16[8,4]{1,0:T(8,128)(2,1)S(1)} %get-tuple-element.109), channel_id=1, source_target_pairs={{1,0},{3,2},{5,4},{7,6},{9,8},{11,10},{13,12},{15,14},{17,16},{19,... | collective-permute-start | bytes 200 | tf_op jit(solution)/shard_map/ppermute | solution.py:42
  105.6 15.1 %collective-permute-start.25 = (bf16[8,4]{1,0:T(8,128)(2,1)S(1)}, bf16[8,4]{1,0:T(8,128)(2,1)S(1)}, u32[]{:S(2)}, u32[]{:S(2)}) collective-permute-start(bf16[8,4]{1,0:T(8,128)(2,1)S(1)} %get-tuple-element.108), channel_id=1, source_target_pairs={{0,1},{2,3},{4,5},{6,7},{8,9},{10,11},{12,13},{14,15},{16,17},{18,... | collective-permute-start | bytes 200 | tf_op jit(solution)/shard_map/ppermute | solution.py:42
  108.7 7.4 %collective-permute-start.20 = (bf16[4,16,1280]{2,1,0:T(8,128)(2,1)S(1)}, bf16[4,16,1280]{2,1,0:T(8,128)(2,1)S(1)}, u32[]{:S(2)}, u32[]{:S(2)}) collective-permute-start(bf16[4,16,1280]{2,1,0:T(8,128)(2,1)S(1)} %bitcast.45), channel_id=1, source_target_pairs={{2,0},{4,2},{6,4},{8,6},{10,8},{12,10},{14,12},{3,1},{5,3},{7,5},{... | collective-permute-start | bytes 491528 | tf_op jit(solution)/shard_map/ppermute | solution.py:42
  116.3 4.4 %collective-permute-start.22 = (bf16[8,4,1280]{2,1,0:T(4,128)(2,1)S(1)}, bf16[8,4,1280]{2,1,0:T(4,128)(2,1)S(1)}, u32[]{:S(2)}, u32[]{:S(2)}) collective-permute-start(bf16[8,4,1280]{2,1,0:T(4,128)(2,1)S(1)} %get-tuple-element.101), channel_id=1, source_target_pairs={{1,0},{3,2},{5,4},{7,6},{9,8},{11,10},{13,12},{15,14},{17,16},{19,... | collective-permute-start | bytes 245768 | tf_op jit(solution)/shard_map/ppermute | solution.py:42
  117.6 3.9 %collective-permute-start.21 = (bf16[8,4,1280]{2,1,0:T(4,128)(2,1)S(1)}, bf16[8,4,1280]{2,1,0:T(4,128)(2,1)S(1)}, u32[]{:S(2)}, u32[]{:S(2)}) collective-permute-start(bf16[8,4,1280]{2,1,0:T(4,128)(2,1)S(1)} %get-tuple-element.100), channel_id=1, source_target_pairs={{0,1},{2,3},{4,5},{6,7},{8,9},{10,11},{12,13},{14,15},{16,17},{18,... | collective-permute-start | bytes 245768 | tf_op jit(solution)/shard_map/ppermute | solution.py:42
Sparse Core Ops, SparseCore 0:
  9.5 63.9 all-gather.1
